TPU v7x, 32 devices: a whole 2x2x4 slice. The times are simulated.
32 devices in a mesh: dp: 2 (over x), row: 4 (over y, core), col: 4 (over z).
Axes of the slice: x: 2, y: 2, z: 4, core: 2. Of those that a mesh axis runs over, the one named last changes fastest.
Arguments:
- inputs: bfloat16 [14568, 12, 128], P(('dp', 'row'), 'col'), may hold values from -15 to 15
- mixer_weight: float32 [768, 2304], P('row', 'col'), may hold values from -0.3125 to 0.3125
- mixer_bias: float32 [12, 128], P('col', 'row'), may hold values from -3 to 3
- merge_weight: float32 [768, 768], P(('col', 'row')), may hold values from -0.875 to 0.875
- merge_bias: float32 [12, 64], P('col', 'row'), may hold values from -3 to 3
- expand_weight: float32 [768, 3072], P('row', 'col'), may hold values from -0.21875 to 0.21875
- expand_bias: float32 [12, 256], P('col', 'row'), may hold values from -3 to 3
- reduce_weight: float32 [3072, 768], P(('col', 'row')), may hold values from -0.109375 to 0.109375
- reduce_bias: float32 [12, 64], P('col', 'row'), may hold values from -3 to 3
- first_gain: float32 [12, 64], P('col', 'row'), may hold values from 0.1 to 1.9
- first_shift: float32 [12, 64], P('col', 'row'), may hold values from -3 to 3
- second_gain: float32 [12, 64], P('col', 'row'), may hold values from 0.1 to 1.9
- second_shift: float32 [12, 64], P('col', 'row'), may hold values from -3 to 3
- cotangent: bfloat16 [14568, 12, 128], P(('dp', 'row'), 'col'), may hold values from -6 to 6
Outputs:
- outputs: bfloat16 [14568, 12, 128], P(('dp', 'row'), 'col')
- input_grad: float32 [14568, 12, 128], P(('dp', 'row'), 'col')
- grad_mixer_weight: float32 [768, 2304], P('row', 'col')
- grad_mixer_bias: float32 [12, 128], P('col', 'row')
- grad_merge_weight: float32 [768, 768], P(('col', 'row'))
- grad_merge_bias: float32 [12, 64], P('col', 'row')
- grad_expand_weight: float32 [768, 3072], P('row', 'col')
- grad_expand_bias: float32 [12, 256], P('col', 'row')
- grad_reduce_weight: float32 [3072, 768], P(('col', 'row'))
- grad_reduce_bias: float32 [12, 64], P('col', 'row')
- grad_first_gain: float32 [12, 64], P('col', 'row')
- grad_first_shift: float32 [12, 64], P('col', 'row')
- grad_second_gain: float32 [12, 64], P('col', 'row')
- grad_second_shift: float32 [12, 64], P('col', 'row')
All inputs are finite; a program needn't handle non-finite values.
Results may differ from a plain program's by a relative error of at most 0.012.
The roundings to bfloat16 on the way count: a program that leaves them out, or rounds other values in their place, can miss the bound.
Values may be sent and summed in bfloat16 or wider, within the bound.
A program may use at most 192 MiB of HBM per device.

v0:
```python
import jax
import jax.numpy as jnp
from jax import lax
from jax.sharding import PartitionSpec as P

D = 768
HD = 64
LEN = 1214
EPSILON = 1e-06


def to_rows(values):
    halves = values.shape[0]
    groups = values.shape[1]
    return (
        values.reshape(halves, groups, 2, HD).transpose(0, 2, 1, 3).reshape(2 * halves, groups * HD)
    )


def from_rows(values):
    halves = values.shape[0] // 2
    groups = values.shape[1] // HD
    return (
        values.reshape(halves, 2, groups, HD).transpose(0, 2, 1, 3).reshape(halves, groups, 2 * HD)
    )


def exact_gelu(values):
    return jax.nn.gelu(values, approximate=False)


def inner_rows(left, right):
    return lax.dot_general(
        left, right, (((0,), (0,)), ((), ())), preferred_element_type=jnp.float32
    )


def times_transposed(left, right):
    return lax.dot_general(
        left, right, (((1,), (1,)), ((), ())), preferred_element_type=jnp.float32
    )


def as_vector(values):
    return values.astype(jnp.float32).reshape(-1)


def row_sum(values):
    return lax.psum(values, "col")


def norm_shard(values, gain, shift):
    centre = row_sum(jnp.sum(values, axis=1)) / D
    centered = values - centre[:, None]
    spread = row_sum(jnp.sum(centered * centered, axis=1)) / D
    inverse = lax.rsqrt(spread + EPSILON)
    scaled = centered * inverse[:, None]
    return (scaled * gain + shift, scaled, inverse)


def spread_rows(values):
    return lax.all_gather(values, "col", axis=1, tiled=True)


def gather_grads(values):
    return lax.all_gather(values, "col", axis=1, tiled=True)


def norm_back(partial_rows, scaled, inverse, gain):
    shard = lax.psum_scatter(partial_rows, "col", scatter_dimension=1, tiled=True)
    grad_gain = jnp.sum(shard * scaled, axis=0)
    grad_shift = jnp.sum(shard, axis=0)
    upstream = shard * gain
    first_sum, second_sum = lax.psum(
        (jnp.sum(upstream, axis=1), jnp.sum(upstream * scaled, axis=1)), "col"
    )
    result = inverse[:, None] * (
        upstream - first_sum[:, None] / D - scaled * (second_sum[:, None] / D)
    )
    return (result, grad_gain, grad_shift)


def attend(parts):
    query, keyset, valueset = parts
    scores = times_transposed(query, keyset) * HD ** (-0.5)
    highest = jnp.max(scores, axis=1, keepdims=True)
    weights = jnp.exp(scores - highest)
    totals = jnp.sum(weights, axis=1, keepdims=True)
    chances = (weights / totals).astype(jnp.bfloat16)
    result = jnp.dot(chances, valueset, preferred_element_type=jnp.float32)
    return (result.astype(jnp.bfloat16), (highest + jnp.log(totals))[:, 0])


def attend_back(parts):
    query, keyset, valueset, upstream, logsum = parts
    scale = HD ** (-0.5)
    scores = times_transposed(query, keyset) * scale
    chances = jnp.exp(scores - logsum[:, None])
    grad_chances = times_transposed(upstream, valueset)
    grad_value = inner_rows(chances.astype(jnp.bfloat16), upstream)
    inner = jnp.sum(grad_chances * chances, axis=1, keepdims=True)
    grad_scores = (chances * (grad_chances - inner)).astype(jnp.bfloat16)
    grad_query = jnp.dot(grad_scores, keyset, preferred_element_type=jnp.float32) * scale
    grad_key = inner_rows(grad_scores, query) * scale
    return jnp.stack([grad_query, grad_key, grad_value], axis=1).astype(jnp.bfloat16)


def body(
    inputs,
    mixer_weight,
    mixer_bias,
    merge_weight,
    merge_bias,
    expand_weight,
    expand_bias,
    reduce_weight,
    reduce_bias,
    first_gain,
    first_shift,
    second_gain,
    second_shift,
    cotangent,
):
    (
        mixer_mat,
        mixer_vec,
        merge_mat,
        merge_vec,
        expand_mat,
        expand_vec,
        reduce_mat,
        reduce_vec,
        gain_one,
        shift_one,
        gain_two,
        shift_two,
    ) = (
        lax.all_gather(mixer_weight.astype(jnp.bfloat16), "row", axis=0, tiled=True),
        lax.all_gather(mixer_bias.astype(jnp.bfloat16), "row", axis=1, tiled=True),
        lax.all_gather(merge_weight.astype(jnp.bfloat16), "row", axis=0, tiled=True),
        lax.all_gather(merge_bias.astype(jnp.bfloat16), "row", axis=1, tiled=True),
        lax.all_gather(expand_weight.astype(jnp.bfloat16), "row", axis=0, tiled=True),
        lax.all_gather(expand_bias.astype(jnp.bfloat16), "row", axis=1, tiled=True),
        lax.all_gather(reduce_weight.astype(jnp.bfloat16), "row", axis=0, tiled=True),
        lax.all_gather(reduce_bias.astype(jnp.bfloat16), "row", axis=1, tiled=True),
        lax.all_gather(first_gain.astype(jnp.bfloat16), "row", axis=1, tiled=True),
        lax.all_gather(first_shift.astype(jnp.bfloat16), "row", axis=1, tiled=True),
        lax.all_gather(second_gain.astype(jnp.bfloat16), "row", axis=1, tiled=True),
        lax.all_gather(second_shift.astype(jnp.bfloat16), "row", axis=1, tiled=True),
    )
    rows = to_rows(inputs).astype(jnp.float32)
    cotan_rows = to_rows(cotangent)
    tokens = rows.shape[0]
    width = rows.shape[1]
    clips = tokens // LEN
    local_heads = width // HD
    hidden_width = expand_mat.shape[1]
    gain_first = as_vector(gain_one)
    gain_second = as_vector(gain_two)
    normed_one, scaled_one, inverse_one = norm_shard(rows, gain_first, as_vector(shift_one))
    full_one = spread_rows(normed_one.astype(jnp.bfloat16))
    pairs = mixer_vec.astype(jnp.float32).reshape(local_heads, 2, HD)
    full_bias = jnp.stack([pairs[:, 0], jnp.zeros_like(pairs[:, 0]), pairs[:, 1]], axis=1).reshape(
        -1
    )
    mixed = (jnp.dot(full_one, mixer_mat, preferred_element_type=jnp.float32) + full_bias).astype(
        jnp.bfloat16
    )
    blocks = (
        mixed.reshape(clips, LEN, local_heads, 3, HD)
        .transpose(3, 0, 2, 1, 4)
        .reshape(3, clips * local_heads, LEN, HD)
    )
    head_blocks, logsums = lax.map(attend, (blocks[0], blocks[1], blocks[2]))
    heads = (
        head_blocks.reshape(clips, local_heads, LEN, HD)
        .transpose(0, 2, 1, 3)
        .reshape(tokens, width)
    )
    branch = lax.psum_scatter(
        jnp.dot(heads, merge_mat, preferred_element_type=jnp.float32),
        "col",
        scatter_dimension=1,
        tiled=True,
    )
    state = rows + branch + as_vector(merge_vec)
    normed_two, scaled_two, inverse_two = norm_shard(state, gain_second, as_vector(shift_two))
    full_two = spread_rows(normed_two.astype(jnp.bfloat16))
    hidden = jnp.dot(full_two, expand_mat, preferred_element_type=jnp.float32) + as_vector(
        expand_vec
    )
    active = exact_gelu(hidden).astype(jnp.bfloat16)
    down = lax.psum_scatter(
        jnp.dot(active, reduce_mat, preferred_element_type=jnp.float32).astype(jnp.bfloat16),
        "col",
        scatter_dimension=1,
        tiled=True,
    ).astype(jnp.float32)
    outputs = from_rows((state + down + as_vector(reduce_vec)).astype(jnp.bfloat16))
    cotan_full = gather_grads(cotan_rows)
    grad_reduce_mat = inner_rows(active, cotan_full)
    grad_reduce_vec = jnp.sum(cotan_rows.astype(jnp.float32), axis=0)
    grad_active = times_transposed(cotan_full, reduce_mat)
    gelu_pull = jax.vjp(exact_gelu, hidden)[1]
    grad_hidden = gelu_pull(grad_active)[0].astype(jnp.bfloat16)
    grad_expand_mat = inner_rows(full_two, grad_hidden)
    grad_expand_vec = jnp.sum(grad_hidden.astype(jnp.float32), axis=0)
    back_two, grad_gain_two, grad_shift_two = norm_back(
        times_transposed(grad_hidden, expand_mat), scaled_two, inverse_two, gain_second
    )
    grad_state = cotan_rows.astype(jnp.float32) + back_two
    grad_branch = grad_state.astype(jnp.bfloat16)
    branch_full = gather_grads(grad_branch)
    grad_merge_mat = inner_rows(heads, branch_full)
    grad_merge_vec = jnp.sum(grad_branch.astype(jnp.float32), axis=0)
    grad_heads = times_transposed(branch_full, merge_mat).astype(jnp.bfloat16)
    grad_blocks = (
        grad_heads.reshape(clips, LEN, local_heads, HD)
        .transpose(0, 2, 1, 3)
        .reshape(clips * local_heads, LEN, HD)
    )
    mixed_grads = lax.map(attend_back, (blocks[0], blocks[1], blocks[2], grad_blocks, logsums))
    grad_mixed = (
        mixed_grads.reshape(clips, local_heads, LEN, 3, HD)
        .transpose(0, 2, 1, 3, 4)
        .reshape(tokens, 3 * width)
    )
    grad_mixer_mat = inner_rows(full_one, grad_mixed)
    bias_sums = jnp.sum(grad_mixed.astype(jnp.float32), axis=0).reshape(local_heads, 3, HD)
    grad_mixer_vec = jnp.stack([bias_sums[:, 0], bias_sums[:, 2]], axis=1).reshape(
        local_heads, 2 * HD
    )
    back_one, grad_gain_one, grad_shift_one = norm_back(
        times_transposed(grad_mixed, mixer_mat), scaled_one, inverse_one, gain_first
    )
    input_grad = from_rows(grad_state + back_one)
    (
        part_mixer_mat,
        part_mixer_vec,
        part_merge_mat,
        part_merge_vec,
        part_expand_mat,
        part_expand_vec,
        part_reduce_mat,
        part_reduce_vec,
        part_gain_one,
        part_shift_one,
        part_gain_two,
        part_shift_two,
    ) = (
        lax.psum_scatter(grad_mixer_mat, "row", scatter_dimension=0, tiled=True),
        lax.psum_scatter(grad_mixer_vec, "row", scatter_dimension=1, tiled=True),
        lax.psum_scatter(grad_merge_mat, "row", scatter_dimension=0, tiled=True),
        lax.psum_scatter(
            grad_merge_vec.reshape(local_heads, HD), "row", scatter_dimension=1, tiled=True
        ),
        lax.psum_scatter(grad_expand_mat, "row", scatter_dimension=0, tiled=True),
        lax.psum_scatter(
            grad_expand_vec.reshape(local_heads, hidden_width // local_heads),
            "row",
            scatter_dimension=1,
            tiled=True,
        ),
        lax.psum_scatter(grad_reduce_mat, "row", scatter_dimension=0, tiled=True),
        lax.psum_scatter(
            grad_reduce_vec.reshape(local_heads, HD), "row", scatter_dimension=1, tiled=True
        ),
        lax.psum_scatter(
            grad_gain_one.reshape(local_heads, HD), "row", scatter_dimension=1, tiled=True
        ),
        lax.psum_scatter(
            grad_shift_one.reshape(local_heads, HD), "row", scatter_dimension=1, tiled=True
        ),
        lax.psum_scatter(
            grad_gain_two.reshape(local_heads, HD), "row", scatter_dimension=1, tiled=True
        ),
        lax.psum_scatter(
            grad_shift_two.reshape(local_heads, HD), "row", scatter_dimension=1, tiled=True
        ),
    )
    summed = lax.psum(
        (
            part_mixer_mat,
            part_mixer_vec,
            part_merge_mat,
            part_merge_vec,
            part_expand_mat,
            part_expand_vec,
            part_reduce_mat,
            part_reduce_vec,
            part_gain_one,
            part_shift_one,
            part_gain_two,
            part_shift_two,
        ),
        "dp",
    )
    return (
        outputs,
        input_grad,
        summed[0],
        summed[1],
        summed[2],
        summed[3],
        summed[4],
        summed[5],
        summed[6],
        summed[7],
        summed[8],
        summed[9],
        summed[10],
        summed[11],
    )


def solution(mesh):
    in_specs = (
        P(("dp", "row"), "col", None),
        P("row", "col"),
        P("col", "row"),
        P(("col", "row"), None),
        P("col", "row"),
        P("row", "col"),
        P("col", "row"),
        P(("col", "row"), None),
        P("col", "row"),
        P("col", "row"),
        P("col", "row"),
        P("col", "row"),
        P("col", "row"),
        P(("dp", "row"), "col", None),
    )
    out_specs = (
        P(("dp", "row"), "col", None),
        P(("dp", "row"), "col", None),
        P("row", "col"),
        P("col", "row"),
        P(("col", "row"), None),
        P("col", "row"),
        P("row", "col"),
        P("col", "row"),
        P(("col", "row"), None),
        P("col", "row"),
        P("col", "row"),
        P("col", "row"),
        P("col", "row"),
        P("col", "row"),
    )
    return jax.shard_map(body, mesh=mesh, in_specs=in_specs, out_specs=out_specs, check_vma=False)
```

profile of v0, /device:TPU:0, one launch (start us, length us, event | category | flops | bytes accessed | tf_op | source)
XLA Modules:
  0.0 1910.4 jit_solution(16474213476146647296)
XLA Ops:
  26.0 19.2 %psum.140 = f32[3642]{0:T(1024)S(1)} all-reduce(f32[3642]{0:T(1024)S(1)} %reduce_sum.167), channel_id=1, replica_groups=mesh['dp'=2,'row'=4,'col'=4] {'col'}, use_global_device_ids=true, to_apply=%region_1.0 | all-reduce | flops 3642 | bytes 29136 | tf_op jit(solution)/shard_map/psum | solution.py:49
  47.6 15.6 psum.141
  63.2 7.0 copy.134
  70.2 9.2 reshape.237
  96.3 10.2 all_gather.51
  106.5 82.4 %all-gather.15.cloned.1.call-done = bf16[3642,768]{0,1:T(8,128)(2,1)} async-done(((bf16[3642,192]{0,1:T(8,128)(2,1)}), bf16[3642,768]{0,1:T(8,128)(2,1)}) %all-gather.15.cloned.1.call-update) | async-done | bytes 5594128 | tf_op jit(solution)/shard_map/all_gather | solution.py:62
  188.9 8.5 add_convert_fusion.1
  197.5 14.2 reshape.217
  229.9 64.2 %while.22 = (s32[]{:T(128)}, bf16[9,1214,64]{1,2,0:T(8,128)(2,1)}, f32[9,1214]{1,0:T(8,128)}, bf16[9,1214,64]{2,1,0:T(8,128)(2,1)}, bf16[9,1214,64]{2,1,0:T(8,12...) while((s32[]{:T(128)}, bf16[9,1214,64]{1,2,0:T(8,128)(2,1)}, f32[9,1214]{1,0:T(8,128)}, ...), condition=%wide.region_7.8_spmd, body=%wide.region_4.7_spmd.sunk | while | flops 387684832 | bytes 18843696 | solution.py:174
  303.9 7.4 fusion.62
  329.1 173.6 %reduce-scatter.33.cloned.1.call-done = f32[3642,192]{0,1:T(8,128)} async-done(((f32[3642,768]{0,1:T(8,128)}), f32[3642,192]{0,1:T(8,128)}) %reduce-scatter.33.cloned.1.call-update) | async-done | bytes 2797072 | tf_op jit(solution)/shard_map/reduce_scatter | solution.py:180
  505.7 18.5 psum.142
  524.5 15.5 psum.143
  552.7 7.8 reshape.223
  569.6 76.5 %all-gather.17.cloned.1.call-done = bf16[3642,768]{0,1:T(8,128)(2,1)} async-done(((bf16[3642,192]{0,1:T(8,128)(2,1)}), bf16[3642,768]{0,1:T(8,128)(2,1)}) %all-gather.17.cloned.1.call-update) | async-done | bytes 5594128 | tf_op jit(solution)/shard_map/all_gather | solution.py:62
  646.1 11.6 fusion.63
  663.7 107.1 %all-gather.23.cloned.1.call-done = bf16[3642,768]{0,1:T(8,128)(2,1)} async-done(((bf16[3642,192]{0,1:T(8,128)(2,1)}), bf16[3642,768]{0,1:T(8,128)(2,1)}) %all-gather.23.cloned.1.call-update) | async-done | bytes 5594128 | tf_op jit(solution)/shard_map/all_gather | solution.py:66
  770.8 35.6 %convert_reduce_fusion.1 = (f32[768]{0:T(1024)S(1)}, bf16[3642,768]{1,0:T(8,128)(2,1)S(1)}, f32[3642,768]{1,0:T(8,128)}) fusion(f32[3642,768]{1,0:T(8,128)} %fusion.63, f32[768]{0:T(1024)S(1)} %reshape.245, bf16[3642,768]{0,1:T(8,128)(2,1)} %all-gather.23.cloned.1.call-done, bf16[768,768]{1,0:T(8,128)(2,1)} %all-gather.21.cloned.1.call-done), kind=kOutput, calls=%fused_computation.57 | convolution fusion | flops 4506056704 | bytes 34750464 | tf_op jit(solution)/shard_map/dot_general | solution.py:39
  808.7 7.5 fusion.64
  816.5 190.9 %reduce-scatter.37.cloned.1.call-done = f32[3642,192]{0,1:T(8,128)} async-done(((f32[3642,768]{0,1:T(8,128)}), f32[3642,192]{0,1:T(8,128)}) %reduce-scatter.37.cloned.1.call-update) | async-done | bytes 2797072 | tf_op jit(solution)/shard_map/reduce_scatter | solution.py:70
  1011.0 18.8 all-reduce.1
  1034.8 104.1 %all-gather.25.cloned.1.call-done = bf16[3642,768]{0,1:T(8,128)(2,1)} async-done(((bf16[3642,192]{0,1:T(8,128)(2,1)}), bf16[3642,768]{0,1:T(8,128)(2,1)}) %all-gather.25.cloned.1.call-update) | async-done | bytes 5594128 | tf_op jit(solution)/shard_map/all_gather | solution.py:66
  1150.2 102.2 %while.23 = (s32[]{:T(128)}, bf16[9,1214,3,64]{1,3,2,0:T(8,128)(2,1)}, bf16[9,1214,64]{2,1,0:T(8,128)(2,1)}, bf16[9,1214,64]{2,1,0:T(8,128)(2,1)}, f32[9,1214]{1...) while((s32[]{:T(128)}, ...), condition=%wide.region_21.22_spmd, body=%wide.region_19.21_spmd.sunk | while | flops 956805568 | bytes 48504736 | solution.py:222
  1252.4 8.6 copy.207
  1261.0 12.2 reshape.227
  1273.2 9.8 fusion.65
  1288.1 11.1 multiply_convert_fusion.1
  1300.1 8.2 convert_reduce_fusion
  1309.5 10.5 fusion.69
  1320.1 10.5 fusion.68
  1336.1 10.0 fusion.66
  1346.2 9.2 convolution_convert_fusion
  1355.5 118.8 %reduce-scatter.39.cloned.1.call-done = f32[3642,192]{0,1:T(8,128)} async-done(((f32[3642,768]{0,1:T(8,128)}), f32[3642,192]{0,1:T(8,128)}) %reduce-scatter.39.cloned.1.call-update) | async-done | bytes 2797072 | tf_op jit(solution)/shard_map/reduce_scatter | solution.py:70
  1485.8 12.0 reduce-scatter.55.cloned.1.call-done
  1498.6 21.8 %reduce-scatter.53.cloned.1.call-done = f32[64,3]{1,0:T(8,128)} async-done(((f32[256,3]{1,0:T(8,128)}), f32[64,3]{1,0:T(8,128)}) %reduce-scatter.53.cloned.1.call-update) | async-done | bytes 784
  1521.1 21.1 %reduce-scatter.63.cloned.1.call-done = f32[16,3]{1,0:T(8,128)} async-done(((f32[64,3]{1,0:T(8,128)}), f32[16,3]{1,0:T(8,128)}) %reduce-scatter.63.cloned.1.call-update) | async-done | bytes 208
  1543.0 21.2 %reduce-scatter.61.cloned.1.call-done = f32[16,3]{1,0:T(8,128)} async-done(((f32[64,3]{1,0:T(8,128)}), f32[16,3]{1,0:T(8,128)}) %reduce-scatter.61.cloned.1.call-update) | async-done | bytes 208
  1565.0 21.8 %reduce-scatter.51.cloned.1.call-done = f32[16,3]{1,0:T(8,128)} async-done(((f32[64,3]{1,0:T(8,128)}), f32[16,3]{1,0:T(8,128)}) %reduce-scatter.51.cloned.1.call-update) | async-done | bytes 208
  1587.5 21.6 %reduce-scatter.49.cloned.1.call-done = f32[32,3]{1,0:T(8,128)} async-done(((f32[128,3]{1,0:T(8,128)}), f32[32,3]{1,0:T(8,128)}) %reduce-scatter.49.cloned.1.call-update) | async-done | bytes 400
  1610.0 34.6 %reduce-scatter.47.cloned.1.call-done = f32[192,768]{1,0:T(8,128)} async-done(((f32[768,768]{1,0:T(8,128)}), f32[192,768]{1,0:T(8,128)}) %reduce-scatter.47.cloned.1.call-update) | async-done | bytes 589840 | tf_op jit(solution)/shard_map/reduce_scatter | solution.py:264
  1644.6 35.8 %reduce-scatter.45.cloned.1.call-done = f32[192,768]{1,0:T(8,128)} async-done(((f32[768,768]{1,0:T(8,128)}), f32[192,768]{1,0:T(8,128)}) %reduce-scatter.45.cloned.1.call-update) | async-done | bytes 589840 | tf_op jit(solution)/shard_map/reduce_scatter | solution.py:257
  1680.4 25.2 %reduce-scatter.43.cloned.1.call-done = f32[48,768]{1,0:T(8,128)} async-done(((f32[192,768]{1,0:T(8,128)}), f32[48,768]{1,0:T(8,128)}) %reduce-scatter.43.cloned.1.call-update) | async-done | bytes 147472 | tf_op jit(solution)/shard_map/reduce_scatter | solution.py:253
  1705.6 32.8 %reduce-scatter.41.cloned.1.call-done = f32[192,576]{1,0:T(8,128)} async-done(((f32[768,576]{1,0:T(8,128)}), f32[192,576]{1,0:T(8,128)}) %reduce-scatter.41.cloned.1.call-update) | async-done | bytes 442384 | tf_op jit(solution)/shard_map/reduce_scatter | solution.py:251
  1738.4 20.2 %all-reduce = (f32[3642]{0:T(1024)S(1)}, f32[3642]{0:T(1024)S(1)}) all-reduce(f32[3642]{0:T(1024)S(1)} %get-tuple-element.185, f32[3642]{0:T(1024)S(1)} %get-tuple-element.186), channel_id=1, replica_groups=mesh['dp'=2,'row'=4,'col'=4] {'col'}, use_global_device_ids=true, to_apply=%region_26.27 | all-reduce | flops 7284 | bytes 58272 | tf_op jit(solution)/shard_map/psum | solution.py:74
  1758.7 83.7 %reduce-scatter.35.cloned.1.call-done = bf16[3642,192]{0,1:T(8,128)(2,1)} async-done(((bf16[3642,768]{0,1:T(8,128)(2,1)}), bf16[3642,192]{0,1:T(8,128)(2,1)}) %reduce-scatter.35.cloned.1.call-update) | async-done | bytes 1398544 | tf_op jit(solution)/shard_map/reduce_scatter | solution.py:193
  1842.4 6.6 multiply_add_fusion
  1864.1 8.7 reshape.228
  1887.1 8.7 all-reduce.2
  (375 shorter events, 367.6 us)
Async XLA Ops:
  8.0 180.9 %all-gather.15.cloned.1.call-start = ((), (), s32[]{:S(2)}) async-start(), calls=%async_computation.16 | async-start | bytes 7127040 | tf_op jit(solution)/shard_map/all_gather | solution.py:62
  21.2 61.8 %copy-start.25 = (f32[192]{0:T(256)}, f32[192]{0:T(256)S(1)}, u32[]{:S(2)}) copy-start(f32[192]{0:T(256)S(1)} %reshape.238) | copy-start | bytes 2308
  45.1 37.8 %copy-start.14 = (f32[3642]{0:T(1024)}, f32[3642]{0:T(1024)S(1)}, u32[]{:S(2)}) copy-start(f32[3642]{0:T(1024)S(1)} %broadcast_multiply_fusion.5) | copy-start | bytes 43708
  63.2 19.8 %copy-start.16 = (f32[3642]{0:T(1024)}, f32[3642]{0:T(1024)S(1)}, u32[]{:S(2)}) copy-start(f32[3642]{0:T(1024)S(1)} %add_rsqrt_fusion.1) | copy-start | bytes 43708
  83.0 23.5 %copy-start.2 = (f32[3642,192]{0,1:T(8,128)}, f32[3642,192]{0,1:T(8,128)S(1)}, u32[]{:S(2)}) copy-start(f32[3642,192]{0,1:T(8,128)S(1)} %copy.149) | copy-start | bytes 8391172
  83.0 7.2 copy-start.18
  83.0 7.2 copy-start.11
  84.6 418.0 %reduce-scatter.33.cloned.1.call-start = ((), (), s32[]{:S(2)}) async-start(), calls=%async_computation.17 | async-start | bytes 14254080 | tf_op jit(solution)/shard_map/reduce_scatter | solution.py:180
  294.1 17.2 copy-start.3
  311.4 258.2 %all-gather.19.cloned.1.call-start = ((), (), s32[]{:S(2)}) async-start(), calls=%async_computation.19 | async-start | bytes 1474560 | tf_op jit(solution)/shard_map/all_gather | solution.py:142
  313.2 332.9 %all-gather.17.cloned.1.call-start = ((), (), s32[]{:S(2)}) async-start(), calls=%async_computation.18 | async-start | bytes 7127040 | tf_op jit(solution)/shard_map/all_gather | solution.py:62
  323.8 706.2 %copy-start.23 = (f32[192]{0:T(256)}, f32[192]{0:T(256)S(1)}, u32[]{:S(2)}) copy-start(f32[192]{0:T(256)S(1)} %reshape.243) | copy-start | bytes 2308
  505.7 524.3 %copy-start = (f32[3642,192]{0,1:T(8,128)}, f32[3642,192]{0,1:T(8,128)S(1)}, u32[]{:S(2)}) copy-start(f32[3642,192]{0,1:T(8,128)S(1)} %get-tuple-element.238) | copy-start | bytes 8391172
  524.2 505.7 %copy-start.9 = (f32[3642]{0:T(1024)}, f32[3642]{0:T(1024)S(1)}, u32[]{:S(2)}) copy-start(f32[3642]{0:T(1024)S(1)} %broadcast_multiply_fusion.4) | copy-start | bytes 43708
  540.1 489.9 %copy-start.12 = (f32[3642]{0:T(1024)}, f32[3642]{0:T(1024)S(1)}, u32[]{:S(2)}) copy-start(f32[3642]{0:T(1024)S(1)} %add_rsqrt_fusion) | copy-start | bytes 43708
  541.8 121.9 %all-gather.21.cloned.1.call-start = ((), (), s32[]{:S(2)}) async-start(), calls=%async_computation.20 | async-start | bytes 1474560 | tf_op jit(solution)/shard_map/all_gather | solution.py:144
  543.7 227.1 %all-gather.23.cloned.1.call-start = ((), (), s32[]{:S(2)}) async-start(), calls=%async_computation.22 | async-start | bytes 7127040 | tf_op jit(solution)/shard_map/all_gather | solution.py:66
  564.3 443.1 %reduce-scatter.37.cloned.1.call-start = ((), (), s32[]{:S(2)}) async-start(), calls=%async_computation.23 | async-start | bytes 14254080 | tf_op jit(solution)/shard_map/reduce_scatter | solution.py:70
  770.8 38.0 %copy-start.34 = (bf16[768,768]{1,0:T(8,128)(2,1)S(1)}, bf16[768,768]{1,0:T(8,128)(2,1)}, u32[]{:S(2)}) copy-start(bf16[768,768]{1,0:T(8,128)(2,1)} %all-gather.19.cloned.1.call-done) | copy-start | bytes 3538948
  816.3 322.6 %all-gather.25.cloned.1.call-start = ((), (), s32[]{:S(2)}) async-start(), calls=%async_computation.24 | async-start | bytes 7127040 | tf_op jit(solution)/shard_map/all_gather | solution.py:66
  1034.7 439.6 %reduce-scatter.39.cloned.1.call-start = ((), (), s32[]{:S(2)}) async-start(), calls=%async_computation.25 | async-start | bytes 14254080 | tf_op jit(solution)/shard_map/reduce_scatter | solution.py:70
  1261.0 12.2 copy-start.7
  1283.0 214.8 %reduce-scatter.55.cloned.1.call-start = ((), (), s32[]{:S(2)}) async-start(), calls=%async_computation.33 | async-start | bytes 40960
  1285.4 234.9 %reduce-scatter.53.cloned.1.call-start = ((), (), s32[]{:S(2)}) async-start(), calls=%async_computation.32 | async-start | bytes 163840
  1286.3 256.0 %reduce-scatter.63.cloned.1.call-start = ((), (), s32[]{:S(2)}) async-start(), calls=%async_computation.37 | async-start | bytes 40960
  1287.2 277.1 %reduce-scatter.61.cloned.1.call-start = ((), (), s32[]{:S(2)}) async-start(), calls=%async_computation.36 | async-start | bytes 40960
  1288.0 298.7 %reduce-scatter.51.cloned.1.call-start = ((), (), s32[]{:S(2)}) async-start(), calls=%async_computation.31 | async-start | bytes 40960
  1300.0 309.2 %reduce-scatter.49.cloned.1.call-start = ((), (), s32[]{:S(2)}) async-start(), calls=%async_computation.30 | async-start | bytes 81920
  1309.1 335.5 %reduce-scatter.47.cloned.1.call-start = ((), (), s32[]{:S(2)}) async-start(), calls=%async_computation.29 | async-start | bytes 2949120 | tf_op jit(solution)/shard_map/reduce_scatter | solution.py:264
  1320.0 10.6 copy-start.5
  1320.0 360.4 %reduce-scatter.45.cloned.1.call-start = ((), (), s32[]{:S(2)}) async-start(), calls=%async_computation.28 | async-start | bytes 2949120 | tf_op jit(solution)/shard_map/reduce_scatter | solution.py:257
  1330.6 375.0 %reduce-scatter.43.cloned.1.call-start = ((), (), s32[]{:S(2)}) async-start(), calls=%async_computation.27 | async-start | bytes 737280 | tf_op jit(solution)/shard_map/reduce_scatter | solution.py:253
  1335.9 10.3 copy-start.33
  1335.9 402.5 %reduce-scatter.41.cloned.1.call-start = ((), (), s32[]{:S(2)}) async-start(), calls=%async_computation.26 | async-start | bytes 2457600 | tf_op jit(solution)/shard_map/reduce_scatter | solution.py:251
  1346.2 496.2 %reduce-scatter.35.cloned.1.call-start = ((), (), s32[]{:S(2)}) async-start(), calls=%async_computation.21 | async-start | bytes 7127040 | tf_op jit(solution)/shard_map/reduce_scatter | solution.py:193
  1355.4 118.9 %copy-start.15 = (f32[3642]{0:T(1024)S(1)}, f32[3642]{0:T(1024)}, u32[]{:S(2)}) copy-start(f32[3642]{0:T(1024)} %copy-done.14) | copy-start | bytes 43708
  1355.4 118.9 %copy-start.17 = (f32[3642]{0:T(1024)S(1)}, f32[3642]{0:T(1024)}, u32[]{:S(2)}) copy-start(f32[3642]{0:T(1024)} %copy-done.16) | copy-start | bytes 43708
  1355.4 118.9 %copy-start.26 = (f32[192]{0:T(256)S(1)}, f32[192]{0:T(256)}, u32[]{:S(2)}) copy-start(f32[192]{0:T(256)} %copy-done.25) | copy-start | bytes 2308
  1355.4 124.2 %copy-start.32 = (f32[3,16]{1,0:T(4,128)S(1)}, f32[3,16]{1,0:T(4,128)}, u32[]{:S(2)}) copy-start(f32[3,16]{1,0:T(4,128)} %param.26) | copy-start | bytes 580
  1355.4 486.9 %copy-start.1 = (f32[3642,192]{0,1:T(8,128)S(1)}, f32[3642,192]{0,1:T(8,128)}, u32[]{:S(2)}) copy-start(f32[3642,192]{0,1:T(8,128)} %copy-done) | copy-start | bytes 8391172
  1355.4 486.9 %copy-start.10 = (f32[3642]{0:T(1024)S(1)}, f32[3642]{0:T(1024)}, u32[]{:S(2)}) copy-start(f32[3642]{0:T(1024)} %copy-done.9) | copy-start | bytes 43708
  1355.5 486.9 %copy-start.13 = (f32[3642]{0:T(1024)S(1)}, f32[3642]{0:T(1024)}, u32[]{:S(2)}) copy-start(f32[3642]{0:T(1024)} %copy-done.12) | copy-start | bytes 43708
  1355.5 486.9 %copy-start.20 = (f32[3642]{0:T(1024)S(1)}, f32[3642]{0:T(1024)}, u32[]{:S(2)}) copy-start(f32[3642]{0:T(1024)} %copy-done.19) | copy-start | bytes 43708
  1355.5 486.9 %copy-start.22 = (f32[3642]{0:T(1024)S(1)}, f32[3642]{0:T(1024)}, u32[]{:S(2)}) copy-start(f32[3642]{0:T(1024)} %copy-done.21) | copy-start | bytes 43708
  1355.5 486.9 %copy-start.24 = (f32[192]{0:T(256)S(1)}, f32[192]{0:T(256)}, u32[]{:S(2)}) copy-start(f32[192]{0:T(256)} %copy-done.23) | copy-start | bytes 2308
  1355.5 525.1 %reduce-scatter.59.cloned.1.call-start = ((), (), s32[]{:S(2)}) async-start(), calls=%async_computation.35 | async-start | bytes 40960
  1479.6 406.7 %reduce-scatter.57.cloned.1.call-start = ((), (), s32[]{:S(2)}) async-start(), calls=%async_computation.34 | async-start | bytes 40960
  1485.6 410.2 %all-reduce.6.cloned.1.call-start = ((), (), s32[]{:S(2)}) async-start(), calls=%async_computation.38 | async-start | bytes 3637248 | tf_op jit(solution)/shard_map/psum | solution.py:281
  (11 other events, 30.6 us)
Sparse Core Ops, SparseCore 0:
  84.8 104.1 all-gather.14
  311.5 191.0 reduce-scatter.32
  1034.8 104.0 all-gather.24
  1283.1 191.1 reduce-scatter.38
  1477.1 20.6 reduce-scatter.54
  1500.6 19.6 reduce-scatter.52
  1522.7 19.5 reduce-scatter.62
  1544.7 19.5 reduce-scatter.60
  1567.2 19.5 reduce-scatter.50
  1589.6 19.5 reduce-scatter.48
  1611.7 32.8 reduce-scatter.46
  1647.5 32.8 reduce-scatter.44
  1683.5 22.0 reduce-scatter.42
  1708.0 30.3 reduce-scatter.40
  1740.6 101.7 reduce-scatter.34
  1844.6 19.8 reduce-scatter.58
  1866.7 19.5 reduce-scatter.56
Sparse Core Ops, SparseCore 1:
  314.0 15.6 all-gather.18
  541.9 104.1 all-gather.16
  648.1 15.5 all-gather.20
  665.3 105.4 all-gather.22
  816.4 191.0 reduce-scatter.36
  1738.5 56.7 all-reduce.5
where the time goes:
time: 1920 us; the launch traced here: 1910 us
  waiting for transfers between devices  1200 us (62%)
  matrix products  251 us (13%)
  local copies, waits for them, and re-layouts  193 us (10%)
  blocking collectives  175 us (9%)
  other arithmetic  76.7 us (4%)
    reduce_scatter x2, waiting for transfers between devices, norm_back(): lax.psum_scatter(partial_rows, 'col', scatter_dimension=1, tiled=True)  310 us
    all_gather x2, waiting for transfers between devices, gather_grads(): return lax.all_gather(values, 'col', axis=1, tiled=True)  211 us
    reduce_scatter x1, waiting for transfers between devices, body(): lax.psum_scatter(jnp.dot(heads, merge_mat, preferred_element_type=jnp.flo...  174 us
    all_gather x2, waiting for transfers between devices, spread_rows(): return lax.all_gather(values, 'col', axis=1, tiled=True)  159 us
    unnamed x31, waiting for transfers between devices  125 us
    dot_general x31, matrix products, times_transposed(): lax.dot_general(left, right, (((1,), (1,)), ((), ())), preferred_element_...  111 us
    reduce_scatter x1, waiting for transfers between devices, body(): lax.psum_scatter(jnp.dot(active, reduce_mat, preferred_element_type=jnp.f...  83.7 us
    psum x4, blocking collectives, row_sum(): return lax.psum(values, 'col')  68.8 us
  transfers between devices with their start and end apart: 23, of which 20 were waited for; matrix products, arithmetic and copies ran while one was open for 8% of the time, Pallas kernels for 0%

commit v1 on v0

--- a/solution.py
+++ b/solution.py
@@ -1,3 +1,4 @@
+import functools
 import jax
 import jax.numpy as jnp
 from jax import lax
@@ -7,6 +8,25 @@
 HD = 64
 LEN = 1214
 EPSILON = 1e-06
+
+
+def finish_inputs_all(inner_x, bus_axis):
+    near, response = (lax.axis_size(bus_axis), lax.axis_index(bus_axis))
+    next_value, all_rows = (inner_x, 1)
+    while all_rows < near:
+        big = lax.ppermute(
+            next_value,
+            axis_name=bus_axis,
+            perm=[(hop_no, hop_no ^ all_rows) for hop_no in range(near)],
+        )
+        left_arr = jnp.concatenate([next_value, big], axis=1)
+        mid_arr = jnp.concatenate([big, next_value], axis=1)
+        next_value = jnp.where(response & all_rows == 0, left_arr, mid_arr)
+        all_rows = 2 * all_rows
+    return next_value
+
+
+recast_terms = functools.partial(finish_inputs_all, bus_axis="col")
 
 
 def to_rows(values):
@@ -63,7 +83,7 @@
 
 
 def gather_grads(values):
-    return lax.all_gather(values, "col", axis=1, tiled=True)
+    return recast_terms(values)
 
 
 def norm_back(partial_rows, scaled, inverse, gain):

time: 1920 us -> 2030 us (1.057)
  waiting for transfers between devices: 1200 us -> 1270 us
  local copies, waits for them, and re-layouts: 193 us -> 221 us
    ppermute x0 -> x4, waiting for transfers between devices: none -> 366 us  [finish_inputs_all(): lax.ppermute(next_value, axis_name=bus_axis, perm=[(hop_no, hop_no ^ all_...]
    all_gather x2 -> x0, waiting for transfers between devices: 211 us -> none  [gather_grads(): return lax.all_gather(values, 'col', axis=1, tiled=True)]
    all_gather x2, waiting for transfers between devices: 159 us -> 82.4 us  [spread_rows(): return lax.all_gather(values, 'col', axis=1, tiled=True)]
    unnamed x31 -> x29, waiting for transfers between devices: 125 us -> 125 us
  transfers between devices with their start and end apart: 23 -> 25, of which waited for: 20 -> 20; matrix products, arithmetic and copies ran while one was open for 8% -> 9% of each run, Pallas kernels for 0% -> 0%
where the time goes in v1:
time: 2030 us; the launch traced here: 2020 us
  waiting for transfers between devices  1270 us (63%)
  matrix products  255 us (13%)
  local copies, waits for them, and re-layouts  221 us (11%)
  blocking collectives  175 us (9%)
  other arithmetic  81 us (4%)
    ppermute x4, waiting for transfers between devices, finish_inputs_all(): lax.ppermute(next_value, axis_name=bus_axis, perm=[(hop_no, hop_no ^ all_...  366 us
    reduce_scatter x2, waiting for transfers between devices, norm_back(): lax.psum_scatter(partial_rows, 'col', scatter_dimension=1, tiled=True)  309 us
    reduce_scatter x1, waiting for transfers between devices, body(): lax.psum_scatter(jnp.dot(heads, merge_mat, preferred_element_type=jnp.flo...  174 us
    unnamed x29, waiting for transfers between devices  125 us
    dot_general x31, matrix products, times_transposed(): lax.dot_general(left, right, (((1,), (1,)), ((), ())), preferred_element_...  114 us
    reduce_scatter x1, waiting for transfers between devices, body(): lax.psum_scatter(jnp.dot(active, reduce_mat, preferred_element_type=jnp.f...  83.9 us
    all_gather x2, waiting for transfers between devices, spread_rows(): return lax.all_gather(values, 'col', axis=1, tiled=True)  82.4 us
    psum x4, blocking collectives, row_sum(): return lax.psum(values, 'col')  68.8 us
  transfers between devices with their start and end apart: 25, of which 20 were waited for; matrix products, arithmetic and copies ran while one was open for 9% of the time, Pallas kernels for 0%

profile of v1, /device:TPU:0, one launch (start us, length us, event | category | flops | bytes accessed | tf_op | source)
XLA Modules:
  0.0 2019.8 jit_solution(11491754327013492149)
XLA Ops:
  26.0 19.2 psum.140
  47.6 15.6 psum.141
  70.2 9.2 reshape.237
  96.3 10.2 all_gather.45
  106.5 82.4 %all-gather.13.cloned.1.call-done = bf16[3642,768]{0,1:T(8,128)(2,1)} async-done(((bf16[3642,192]{0,1:T(8,128)(2,1)}), bf16[3642,768]{0,1:T(8,128)(2,1)}) %all-gather.13.cloned.1.call-update) | async-done | bytes 5594128 | tf_op jit(solution)/shard_map/all_gather | solution.py:82
  188.9 8.5 add_convert_fusion.1
  197.5 14.3 reshape.217
  230.0 64.2 %while.22 = (s32[]{:T(128)}, bf16[9,1214,64]{1,2,0:T(8,128)(2,1)}, f32[9,1214]{1,0:T(8,128)}, bf16[9,1214,64]{2,1,0:T(8,128)(2,1)}, bf16[9,1214,64]{2,1,0:T(8,12...) while((s32[]{:T(128)}, bf16[9,1214,64]{1,2,0:T(8,128)(2,1)}, f32[9,1214]{1,0:T(8,128)}, ...), condition=%wide.region_7.8_spmd, body=%wide.region_4.7_spmd.sunk | while | flops 387684832 | bytes 18843696 | solution.py:194
  304.1 7.4 fusion.69
  329.3 173.6 %reduce-scatter.33.cloned.1.call-done = f32[3642,192]{0,1:T(8,128)} async-done(((f32[3642,768]{0,1:T(8,128)}), f32[3642,192]{0,1:T(8,128)}) %reduce-scatter.33.cloned.1.call-update) | async-done | bytes 2797072 | tf_op jit(solution)/shard_map/reduce_scatter | solution.py:200
  505.9 18.5 psum.142
  524.8 15.5 psum.143
  550.6 7.9 reshape.223
  562.3 103.1 %collective-permute-done = bf16[3642,192]{0,1:T(8,128)(2,1)} collective-permute-done((bf16[3642,192]{0,1:T(8,128)(2,1)}, bf16[3642,192]{0,1:T(8,128)(2,1)}, u32[]{:S(2)}, u32[]{:S(2)}) %collective-permute-start) | collective-permute-done | bytes 1398560 | tf_op jit(solution)/shard_map/ppermute | solution.py:17
  681.4 115.1 %collective-permute-done.1 = bf16[3642,384]{1,0:T(8,128)(2,1)} collective-permute-done((bf16[3642,384]{1,0:T(8,128)(2,1)}, bf16[3642,384]{1,0:T(8,128)(2,1)}, u32[]{:S(2)}, u32[]{:S(2)}) %collective-permute-start.1) | collective-permute-done | bytes 2797088 | tf_op jit(solution)/shard_map/ppermute | solution.py:17
  796.5 13.4 copy.178
  809.9 11.6 fusion.70
  821.5 36.7 %convert_reduce_fusion.1 = (f32[768]{0:T(1024)S(1)}, bf16[3642,768]{1,0:T(8,128)(2,1)S(1)}, f32[3642,768]{1,0:T(8,128)}) fusion(f32[3642,768]{1,0:T(8,128)} %fusion.70, f32[768]{0:T(1024)S(1)} %reshape.245, bf16[768,768]{1,0:T(8,128)(2,1)} %all-gather.19.cloned.1.call-done, bf16[3642,384]{0,1:T(8,128)(2,1)} %copy.178, ...), kind=kOutput, calls=%fused_computation.57 | convolution fusion | flops 4531229696 | bytes 34750464 | tf_op jit(solution)/shard_map/dot_general | solution.py:59
  860.6 7.5 fusion.71
  868.2 191.1 %reduce-scatter.37.cloned.1.call-done = f32[3642,192]{0,1:T(8,128)} async-done(((f32[3642,768]{0,1:T(8,128)}), f32[3642,192]{0,1:T(8,128)}) %reduce-scatter.37.cloned.1.call-update) | async-done | bytes 2797072 | tf_op jit(solution)/shard_map/reduce_scatter | solution.py:90
  1063.0 19.1 all-reduce.1
  1085.9 29.3 %collective-permute-done.2 = bf16[3642,192]{0,1:T(8,128)(2,1)S(1)} collective-permute-done((bf16[3642,192]{0,1:T(8,128)(2,1)S(1)}, bf16[3642,192]{0,1:T(8,128)(2,1)S(1)}, u32[]{:S(2)}, u32[]{:S(2)}) %collective-permute-start.2) | collective-permute-done | bytes 1398560 | tf_op jit(solution)/shard_map/ppermute | solution.py:17
  1120.2 118.6 %collective-permute-done.3 = bf16[3642,384]{1,0:T(8,128)(2,1)} collective-permute-done((bf16[3642,384]{1,0:T(8,128)(2,1)}, bf16[3642,384]{1,0:T(8,128)(2,1)}, u32[]{:S(2)}, u32[]{:S(2)}) %collective-permute-start.3) | collective-permute-done | bytes 2797088 | tf_op jit(solution)/shard_map/ppermute | solution.py:17
  1259.2 102.6 %while.23 = (s32[]{:T(128)}, bf16[9,1214,3,64]{1,3,2,0:T(8,128)(2,1)}, bf16[9,1214,64]{2,1,0:T(8,128)(2,1)}, bf16[9,1214,64]{2,1,0:T(8,128)(2,1)}, f32[9,1214]{1...) while((s32[]{:T(128)}, ...), condition=%wide.region_21.22_spmd, body=%wide.region_19.21_spmd.sunk | while | flops 956805568 | bytes 48504736 | solution.py:242
  1361.9 8.6 copy.229
  1370.4 12.2 reshape.227
  1382.6 9.6 fusion.72
  1397.3 10.9 multiply_convert_fusion.1
  1409.2 8.2 convert_reduce_fusion
  1418.3 10.6 fusion.54
  1429.2 10.5 fusion.74
  1445.6 9.9 fusion.73
  1455.6 9.2 convolution_convert_fusion
  1465.2 117.9 %reduce-scatter.39.cloned.1.call-done = f32[3642,192]{0,1:T(8,128)} async-done(((f32[3642,768]{0,1:T(8,128)}), f32[3642,192]{0,1:T(8,128)}) %reduce-scatter.39.cloned.1.call-update) | async-done | bytes 2797072 | tf_op jit(solution)/shard_map/reduce_scatter | solution.py:90
  1594.6 12.0 reduce-scatter.55.cloned.1.call-done
  1607.3 21.7 %reduce-scatter.53.cloned.1.call-done = f32[64,3]{1,0:T(8,128)} async-done(((f32[256,3]{1,0:T(8,128)}), f32[64,3]{1,0:T(8,128)}) %reduce-scatter.53.cloned.1.call-update) | async-done | bytes 784
  1629.9 21.0 %reduce-scatter.63.cloned.1.call-done = f32[16,3]{1,0:T(8,128)} async-done(((f32[64,3]{1,0:T(8,128)}), f32[16,3]{1,0:T(8,128)}) %reduce-scatter.63.cloned.1.call-update) | async-done | bytes 208
  1651.7 21.2 %reduce-scatter.61.cloned.1.call-done = f32[16,3]{1,0:T(8,128)} async-done(((f32[64,3]{1,0:T(8,128)}), f32[16,3]{1,0:T(8,128)}) %reduce-scatter.61.cloned.1.call-update) | async-done | bytes 208
  1673.7 21.8 %reduce-scatter.51.cloned.1.call-done = f32[16,3]{1,0:T(8,128)} async-done(((f32[64,3]{1,0:T(8,128)}), f32[16,3]{1,0:T(8,128)}) %reduce-scatter.51.cloned.1.call-update) | async-done | bytes 208
  1696.2 21.9 %reduce-scatter.49.cloned.1.call-done = f32[32,3]{1,0:T(8,128)} async-done(((f32[128,3]{1,0:T(8,128)}), f32[32,3]{1,0:T(8,128)}) %reduce-scatter.49.cloned.1.call-update) | async-done | bytes 400
  1718.8 34.4 %reduce-scatter.47.cloned.1.call-done = f32[192,768]{1,0:T(8,128)} async-done(((f32[768,768]{1,0:T(8,128)}), f32[192,768]{1,0:T(8,128)}) %reduce-scatter.47.cloned.1.call-update) | async-done | bytes 589840 | tf_op jit(solution)/shard_map/reduce_scatter | solution.py:284
  1753.3 36.0 %reduce-scatter.45.cloned.1.call-done = f32[192,768]{1,0:T(8,128)} async-done(((f32[768,768]{1,0:T(8,128)}), f32[192,768]{1,0:T(8,128)}) %reduce-scatter.45.cloned.1.call-update) | async-done | bytes 589840 | tf_op jit(solution)/shard_map/reduce_scatter | solution.py:277
  1789.2 25.1 %reduce-scatter.43.cloned.1.call-done = f32[48,768]{1,0:T(8,128)} async-done(((f32[192,768]{1,0:T(8,128)}), f32[48,768]{1,0:T(8,128)}) %reduce-scatter.43.cloned.1.call-update) | async-done | bytes 147472 | tf_op jit(solution)/shard_map/reduce_scatter | solution.py:273
  1814.3 32.9 %reduce-scatter.41.cloned.1.call-done = f32[192,576]{1,0:T(8,128)} async-done(((f32[768,576]{1,0:T(8,128)}), f32[192,576]{1,0:T(8,128)}) %reduce-scatter.41.cloned.1.call-update) | async-done | bytes 442384 | tf_op jit(solution)/shard_map/reduce_scatter | solution.py:271
  1847.2 20.0 all-reduce
  1867.2 83.9 %reduce-scatter.35.cloned.1.call-done = bf16[3642,192]{0,1:T(8,128)(2,1)} async-done(((bf16[3642,768]{0,1:T(8,128)(2,1)}), bf16[3642,192]{0,1:T(8,128)(2,1)}) %reduce-scatter.35.cloned.1.call-update) | async-done | bytes 1398544 | tf_op jit(solution)/shard_map/reduce_scatter | solution.py:213
  1972.9 8.7 reshape.228
  1996.0 8.7 all-reduce.2
  (387 shorter events, 397.3 us)
Async XLA Ops:
  8.0 180.9 %all-gather.13.cloned.1.call-start = ((), (), s32[]{:S(2)}) async-start(), calls=%async_computation.16 | async-start | bytes 7127040 | tf_op jit(solution)/shard_map/all_gather | solution.py:82
  21.2 61.8 %copy-start.27 = (f32[192]{0:T(256)}, f32[192]{0:T(256)S(1)}, u32[]{:S(2)}) copy-start(f32[192]{0:T(256)S(1)} %reshape.238) | copy-start | bytes 2308
  45.1 37.8 %copy-start.16 = (f32[3642]{0:T(1024)}, f32[3642]{0:T(1024)S(1)}, u32[]{:S(2)}) copy-start(f32[3642]{0:T(1024)S(1)} %broadcast_multiply_fusion.5) | copy-start | bytes 43708
  63.2 19.8 copy-start.18
  83.0 114.5 %copy-start.2 = (f32[3642,192]{0,1:T(8,128)}, f32[3642,192]{0,1:T(8,128)S(1)}, u32[]{:S(2)}) copy-start(f32[3642,192]{0,1:T(8,128)S(1)} %copy.163) | copy-start | bytes 8391172
  84.6 418.2 %reduce-scatter.33.cloned.1.call-start = ((), (), s32[]{:S(2)}) async-start(), calls=%async_computation.17 | async-start | bytes 14254080 | tf_op jit(solution)/shard_map/reduce_scatter | solution.py:200
  294.2 17.3 copy-start.3
  311.6 498.3 %all-gather.17.cloned.1.call-start = ((), (), s32[]{:S(2)}) async-start(), calls=%async_computation.19 | async-start | bytes 1474560 | tf_op jit(solution)/shard_map/all_gather | solution.py:162
  313.4 496.6 %all-gather.15.cloned.1.call-start = ((), (), s32[]{:S(2)}) async-start(), calls=%async_computation.18 | async-start | bytes 7127040 | tf_op jit(solution)/shard_map/all_gather | solution.py:82
  323.9 758.2 %copy-start.25 = (f32[192]{0:T(256)}, f32[192]{0:T(256)S(1)}, u32[]{:S(2)}) copy-start(f32[192]{0:T(256)S(1)} %reshape.243) | copy-start | bytes 2308
  505.9 576.3 %copy-start = (f32[3642,192]{0,1:T(8,128)}, f32[3642,192]{0,1:T(8,128)S(1)}, u32[]{:S(2)}) copy-start(f32[3642,192]{0,1:T(8,128)S(1)} %get-tuple-element.238) | copy-start | bytes 8391172
  524.4 557.8 %copy-start.11 = (f32[3642]{0:T(1024)}, f32[3642]{0:T(1024)S(1)}, u32[]{:S(2)}) copy-start(f32[3642]{0:T(1024)S(1)} %broadcast_multiply_fusion.4) | copy-start | bytes 43708
  540.3 541.9 %copy-start.14 = (f32[3642]{0:T(1024)}, f32[3642]{0:T(1024)S(1)}, u32[]{:S(2)}) copy-start(f32[3642]{0:T(1024)S(1)} %add_rsqrt_fusion) | copy-start | bytes 43708
  542.0 279.6 %all-gather.19.cloned.1.call-start = ((), (), s32[]{:S(2)}) async-start(), calls=%async_computation.20 | async-start | bytes 1474560 | tf_op jit(solution)/shard_map/all_gather | solution.py:164
  562.2 103.2 %collective-permute-start = (bf16[3642,192]{0,1:T(8,128)(2,1)}, bf16[3642,192]{0,1:T(8,128)(2,1)}, u32[]{:S(2)}, u32[]{:S(2)}) collective-permute-start(bf16[3642,192]{0,1:T(8,128)(2,1)} %copy.173), channel_id=1, source_target_pairs={{0,1},{1,0},{2,3},{3,2},{4,5},{5,4},{6,7},{7,6},{8,9},{9,8},{10,11... | collective-permute-start | bytes 4195592 | tf_op jit(solution)/shard_map/ppermute | solution.py:17
  674.3 122.2 %collective-permute-start.1 = (bf16[3642,384]{1,0:T(8,128)(2,1)}, bf16[3642,384]{1,0:T(8,128)(2,1)}, u32[]{:S(2)}, u32[]{:S(2)}) collective-permute-start(bf16[3642,384]{1,0:T(8,128)(2,1)} %copy.177), channel_id=1, source_target_pairs={{0,2},{1,3},{2,0},{3,1},{4,6},{5,7},{6,4},{7,5},{8,10},{9,11},{10,... | collective-permute-start | bytes 8391176 | tf_op jit(solution)/shard_map/ppermute | solution.py:17
  676.1 383.3 %reduce-scatter.37.cloned.1.call-start = ((), (), s32[]{:S(2)}) async-start(), calls=%async_computation.22 | async-start | bytes 14254080 | tf_op jit(solution)/shard_map/reduce_scatter | solution.py:90
  821.5 39.1 %copy-start.36 = (bf16[768,768]{1,0:T(8,128)(2,1)S(1)}, bf16[768,768]{1,0:T(8,128)(2,1)}, u32[]{:S(2)}) copy-start(bf16[768,768]{1,0:T(8,128)(2,1)} %all-gather.17.cloned.1.call-done) | copy-start | bytes 3538948
  868.2 714.9 %reduce-scatter.39.cloned.1.call-start = ((), (), s32[]{:S(2)}) async-start(), calls=%async_computation.23 | async-start | bytes 14254080 | tf_op jit(solution)/shard_map/reduce_scatter | solution.py:90
  1085.8 29.4 %collective-permute-start.2 = (bf16[3642,192]{0,1:T(8,128)(2,1)S(1)}, bf16[3642,192]{0,1:T(8,128)(2,1)S(1)}, u32[]{:S(2)}, u32[]{:S(2)}) collective-permute-start(bf16[3642,192]{0,1:T(8,128)(2,1)S(1)} %get-tuple-element.236), channel_id=1, source_target_pairs={{0,1},{1,0},{2,3},{3,2},{4,5},{5,4},{6,7},{7,6},{8,9},{9,8},{10,11... | collective-permute-start | bytes 4195592 | tf_op jit(solution)/shard_map/ppermute | solution.py:17
  1116.5 126.9 %copy-start.6 = (bf16[3642,384]{0,1:T(8,128)(2,1)}, bf16[3642,384]{0,1:T(8,128)(2,1)S(1)}, u32[]{:S(2)}) copy-start(bf16[3642,384]{0,1:T(8,128)(2,1)S(1)} %maximum_select_fusion.3) | copy-start | bytes 8391172
  1119.6 119.2 %collective-permute-start.3 = (bf16[3642,384]{1,0:T(8,128)(2,1)}, bf16[3642,384]{1,0:T(8,128)(2,1)}, u32[]{:S(2)}, u32[]{:S(2)}) collective-permute-start(bf16[3642,384]{1,0:T(8,128)(2,1)} %copy.180), channel_id=1, source_target_pairs={{0,2},{1,3},{2,0},{3,1},{4,6},{5,7},{6,4},{7,5},{8,10},{9,11},{10,... | collective-permute-start | bytes 8391176 | tf_op jit(solution)/shard_map/ppermute | solution.py:17
  1370.4 12.2 copy-start.9
  1392.3 214.3 %reduce-scatter.55.cloned.1.call-start = ((), (), s32[]{:S(2)}) async-start(), calls=%async_computation.31 | async-start | bytes 40960
  1394.6 234.4 %reduce-scatter.53.cloned.1.call-start = ((), (), s32[]{:S(2)}) async-start(), calls=%async_computation.30 | async-start | bytes 163840
  1395.5 255.4 %reduce-scatter.63.cloned.1.call-start = ((), (), s32[]{:S(2)}) async-start(), calls=%async_computation.35 | async-start | bytes 40960
  1396.4 276.5 %reduce-scatter.61.cloned.1.call-start = ((), (), s32[]{:S(2)}) async-start(), calls=%async_computation.34 | async-start | bytes 40960
  1397.3 298.2 %reduce-scatter.51.cloned.1.call-start = ((), (), s32[]{:S(2)}) async-start(), calls=%async_computation.29 | async-start | bytes 40960
  1409.0 309.0 %reduce-scatter.49.cloned.1.call-start = ((), (), s32[]{:S(2)}) async-start(), calls=%async_computation.28 | async-start | bytes 81920
  1418.2 335.0 %reduce-scatter.47.cloned.1.call-start = ((), (), s32[]{:S(2)}) async-start(), calls=%async_computation.27 | async-start | bytes 2949120 | tf_op jit(solution)/shard_map/reduce_scatter | solution.py:284
  1428.9 10.9 copy-start.7
  1428.9 360.3 %reduce-scatter.45.cloned.1.call-start = ((), (), s32[]{:S(2)}) async-start(), calls=%async_computation.26 | async-start | bytes 2949120 | tf_op jit(solution)/shard_map/reduce_scatter | solution.py:277
  1439.7 374.5 %reduce-scatter.43.cloned.1.call-start = ((), (), s32[]{:S(2)}) async-start(), calls=%async_computation.25 | async-start | bytes 737280 | tf_op jit(solution)/shard_map/reduce_scatter | solution.py:273
  1445.6 401.7 %reduce-scatter.41.cloned.1.call-start = ((), (), s32[]{:S(2)}) async-start(), calls=%async_computation.24 | async-start | bytes 2457600 | tf_op jit(solution)/shard_map/reduce_scatter | solution.py:271
  1455.6 495.6 %reduce-scatter.35.cloned.1.call-start = ((), (), s32[]{:S(2)}) async-start(), calls=%async_computation.21 | async-start | bytes 7127040 | tf_op jit(solution)/shard_map/reduce_scatter | solution.py:213
  1464.8 118.3 %copy-start.17 = (f32[3642]{0:T(1024)S(1)}, f32[3642]{0:T(1024)}, u32[]{:S(2)}) copy-start(f32[3642]{0:T(1024)} %copy-done.16) | copy-start | bytes 43708
  1464.8 118.3 %copy-start.19 = (f32[3642]{0:T(1024)S(1)}, f32[3642]{0:T(1024)}, u32[]{:S(2)}) copy-start(f32[3642]{0:T(1024)} %copy-done.18) | copy-start | bytes 43708
  1464.8 118.3 %copy-start.28 = (f32[192]{0:T(256)S(1)}, f32[192]{0:T(256)}, u32[]{:S(2)}) copy-start(f32[192]{0:T(256)} %copy-done.27) | copy-start | bytes 2308
  1464.8 123.6 %copy-start.34 = (f32[3,16]{1,0:T(4,128)S(1)}, f32[3,16]{1,0:T(4,128)}, u32[]{:S(2)}) copy-start(f32[3,16]{1,0:T(4,128)} %param.26) | copy-start | bytes 580
  1464.8 486.4 %copy-start.1 = (f32[3642,192]{0,1:T(8,128)S(1)}, f32[3642,192]{0,1:T(8,128)}, u32[]{:S(2)}) copy-start(f32[3642,192]{0,1:T(8,128)} %copy-done) | copy-start | bytes 8391172
  1464.8 486.4 %copy-start.12 = (f32[3642]{0:T(1024)S(1)}, f32[3642]{0:T(1024)}, u32[]{:S(2)}) copy-start(f32[3642]{0:T(1024)} %copy-done.11) | copy-start | bytes 43708
  1464.8 486.4 %copy-start.15 = (f32[3642]{0:T(1024)S(1)}, f32[3642]{0:T(1024)}, u32[]{:S(2)}) copy-start(f32[3642]{0:T(1024)} %copy-done.14) | copy-start | bytes 43708
  1464.9 486.3 %copy-start.22 = (f32[3642]{0:T(1024)S(1)}, f32[3642]{0:T(1024)}, u32[]{:S(2)}) copy-start(f32[3642]{0:T(1024)} %copy-done.21) | copy-start | bytes 43708
  1464.9 486.3 %copy-start.24 = (f32[3642]{0:T(1024)S(1)}, f32[3642]{0:T(1024)}, u32[]{:S(2)}) copy-start(f32[3642]{0:T(1024)} %copy-done.23) | copy-start | bytes 43708
  1464.9 486.3 %copy-start.26 = (f32[192]{0:T(256)S(1)}, f32[192]{0:T(256)}, u32[]{:S(2)}) copy-start(f32[192]{0:T(256)} %copy-done.25) | copy-start | bytes 2308
  1464.9 524.5 %reduce-scatter.59.cloned.1.call-start = ((), (), s32[]{:S(2)}) async-start(), calls=%async_computation.33 | async-start | bytes 40960
  1588.4 406.9 %reduce-scatter.57.cloned.1.call-start = ((), (), s32[]{:S(2)}) async-start(), calls=%async_computation.32 | async-start | bytes 40960
  1594.3 410.4 %all-reduce.6.cloned.1.call-start = ((), (), s32[]{:S(2)}) async-start(), calls=%async_computation.36 | async-start | bytes 3637248 | tf_op jit(solution)/shard_map/psum | solution.py:301
  (15 other events, 65.5 us)
Sparse Core Ops, SparseCore 0:
  84.8 104.1 all-gather.12
  311.7 191.0 reduce-scatter.32
  1392.4 190.6 reduce-scatter.38
  1585.9 20.5 reduce-scatter.54
  1609.4 19.6 reduce-scatter.52
  1631.3 19.5 reduce-scatter.62
  1653.3 19.5 reduce-scatter.60
  1675.9 19.5 reduce-scatter.50
  1698.4 19.5 reduce-scatter.48
  1720.4 32.7 reduce-scatter.46
  1756.4 32.8 reduce-scatter.44
  1792.1 22.0 reduce-scatter.42
  1816.8 30.3 reduce-scatter.40
  1849.4 101.7 reduce-scatter.34
  1953.4 19.9 reduce-scatter.58
  1975.7 19.5 reduce-scatter.56
Sparse Core Ops, SparseCore 1:
  314.2 15.6 all-gather.16
  542.1 132.5 all-gather.14
  676.6 17.9 all-gather.18
  868.3 191.1 reduce-scatter.36
  1847.3 56.7 all-reduce.5
